TPU v7x, 512 devices: a whole 4x4x16 slice. The times are simulated.
512 devices in a mesh: tm: 8 (over y, core), space: 64 (over z, x).
Axes of the slice: x: 4, y: 4, z: 16, core: 2. Of those that a mesh axis runs over, the one named last changes fastest.
Arguments:
- snapshots: bfloat16 [128, 128, 16384], P('tm', None, 'space'), as said below
- frequencies: int32 [16], replicated, may hold values from 1 to 63, as said below
- offsets: int32 [128], P('tm'), may hold values from 0 to 16383
Outputs:
- modes: float32 [16, 2, 128, 16384], P('tm', None, None, 'space')
Inputs may be any that keep to these rules, and one draw needn't show every extreme that they name: `frequencies`: the kept frequency indices are distinct and include 1 and 63. `snapshots`: snapshot values of the record.
All inputs are finite; a program needn't handle non-finite values.
Results may differ from a plain program's by a relative error of at most 0.0041.
Values may be sent and summed in bfloat16 or wider, within the bound.
A program may use at most 64 MiB of HBM per device.

v0:
```python
import math
import jax
import jax.numpy as jnp
from jax import lax
from jax.sharding import PartitionSpec as P


def make_angle_table(frequencies, length):
    positions = jnp.arange(length, dtype=jnp.int32)
    turn_counts = frequencies[None, :] * positions[:, None] % length
    radians = turn_counts.astype(jnp.float32) * (2.0 * math.pi / length)
    window = 0.5 - 0.5 * jnp.cos(positions.astype(jnp.float32) * (2.0 * math.pi / length))
    cosine_cols = window[:, None] * jnp.cos(radians)
    sine_cols = window[:, None] * jnp.sin(radians)
    return jnp.concatenate([cosine_cols, sine_cols], axis=1).astype(jnp.bfloat16)


def embed_gram(gram_real, gram_imag):
    top_rows = jnp.stack([gram_real, -gram_imag], axis=-1)
    low_rows = jnp.stack([gram_imag, gram_real], axis=-1)
    order = gram_real.shape[0]
    return jnp.stack([top_rows, low_rows], axis=1).reshape(2 * order, 2 * order)


def local_gram(real_rows, imag_rows):
    real_gram = jnp.dot(real_rows, real_rows.T, preferred_element_type=jnp.float32) + jnp.dot(
        imag_rows, imag_rows.T, preferred_element_type=jnp.float32
    )
    cross = jnp.dot(imag_rows, real_rows.T, preferred_element_type=jnp.float32)
    imag_gram = cross - cross.T
    return jnp.stack([real_gram, imag_gram])


def unpack_gram(packed):
    return (packed[0], packed[1])


def finish_modes(packed, real_rows, imag_rows, total_cells):
    gram_real, gram_imag = unpack_gram(packed)
    embedded = embed_gram(gram_real / total_cells, gram_imag / total_cells)
    lower_factor = jnp.linalg.cholesky(embedded)
    order = real_rows.shape[0]
    cells_here = real_rows.shape[1]
    stacked_rows = (
        jnp.stack([real_rows, imag_rows], axis=1).reshape(2 * order, cells_here).astype(jnp.float32)
    )
    solved = lax.linalg.triangular_solve(lower_factor, stacked_rows, left_side=True, lower=True)
    return jnp.transpose(solved.reshape(order, 2, cells_here), (1, 0, 2))


def local(snapshots, frequencies, offsets):
    length = snapshots.shape[1]
    count_all = frequencies.shape[0]
    angle_table = make_angle_table(frequencies, length)
    projected = jnp.einsum(
        "btc,tk->kbc", snapshots, angle_table, preferred_element_type=jnp.float32
    )
    cos_part = projected[:count_all]
    sin_part = projected[count_all:]
    turn_counts = frequencies[:, None] * offsets[None, :] % length
    phase = turn_counts.astype(jnp.float32) * (2.0 * math.pi / length)
    cos_phase = jnp.cos(phase)[:, :, None]
    sin_phase = jnp.sin(phase)[:, :, None]
    real_part = cos_part * cos_phase - sin_part * sin_phase
    imag_part = -(sin_part * cos_phase + cos_part * sin_phase)
    stacked = jnp.stack([real_part, imag_part]).astype(jnp.bfloat16)
    regrouped = lax.all_to_all(stacked, "tm", split_axis=1, concat_axis=2, tiled=True)
    cells_here = regrouped.shape[3]
    total_cells = cells_here * lax.axis_size("space")
    per_freq = [
        (regrouped[0, slot_index], regrouped[1, slot_index])
        for slot_index in range(regrouped.shape[1])
    ]
    local_grams = jnp.stack([local_gram(real_rows, imag_rows) for real_rows, imag_rows in per_freq])
    summed = lax.psum(local_grams, "space")
    results = [
        finish_modes(
            summed[slot_index], per_freq[slot_index][0], per_freq[slot_index][1], total_cells
        )
        for slot_index in range(len(per_freq))
    ]
    return jnp.stack(results)


def solution(mesh):
    placed = (P("tm", None, "space"), P(), P("tm"))
    return jax.shard_map(
        local, mesh=mesh, in_specs=placed, out_specs=P("tm", None, None, "space"), check_vma=False
    )
```

profile of v0, /device:TPU:8, one launch (start us, length us, event | category | flops | bytes accessed | tf_op | source)
XLA Modules:
  0.0 465.1 jit_solution(17110627762532385624)
XLA Ops:
  6.6 0.9 multiply_convert_fusion.1
  7.5 0.8 fusion.59
  8.3 0.3 fusion.52
  8.7 0.8 copy.34
  9.5 9.1 %all-to-all-start = ((bf16[2,16,16,256]{3,2,0,1:T(8,128)(2,1)}), bf16[2,16,16,256]{3,2,0,1:T(8,128)(2,1)S(1)}, u32[]{:S(2)}, u32[]{:S(2)}) async-start(bf16[2,16,16,256]{3,2,0,1:T(8,128)(2,1)} %copy.34), calls=%async_computation | async-start | bytes 524288 | tf_op jit(solution)/shard_map/all_to_all | solution.py:67
  18.7 6.1 %all-to-all-done = bf16[2,16,16,256]{3,2,0,1:T(8,128)(2,1)S(1)} async-done(((bf16[2,16,16,256]{3,2,0,1:T(8,128)(2,1)}), bf16[2,16,16,256]{3,2,0,1:T(8,128)(2,1)S(1)}, u32[]{:S(2)}, u32[]{:S(2)}) %all-to-all-start) | async-done | bytes 262176 | tf_op jit(solution)/shard_map/all_to_all | solution.py:67
  26.0 0.7 pad_maximum_fusion.2
  26.9 0.2 copy.41
  27.3 0.2 copy.45
  27.7 261.0 %all-reduce.3.cloned.1.call-done = f32[2,2,128,128]{3,2,1,0:T(8,128)} async-done(((f32[2,2,128,128]{3,2,1,0:T(8,128)}), f32[2,2,128,128]{3,2,1,0:T(8,128)}) %all-reduce.3.cloned.1.call-update) | async-done | bytes 262160 | tf_op jit(solution)/shard_map/psum | solution.py:75
  288.7 1.0 fusion.20
  289.6 0.9 fusion.61
  290.6 8.8 %copy.39 = f32[128,2,128,2]{3,2,1,0:T(8,128)} copy(f32[128,2,128,2]{2,0,3,1:T(8,128)S(1)} %pad_maximum_fusion.3) | data formatting | bytes 524288 | tf_op jit(solution)/shard_map/stack | solution.py:22
  299.4 12.7 %reshape.178 = f32[256,256]{1,0:T(8,128)S(1)} reshape(f32[128,2,128,2]{3,2,1,0:T(8,128)} %copy.39) | data formatting | bytes 524288 | tf_op jit(solution)/shard_map/reshape | solution.py:22
  312.3 11.7 %cholesky.130 = f32[128,128]{1,0:T(8,128)S(1)} custom-call(f32[128,128]{1,0:T(8,128)S(1)} %cholesky.194), custom_call_target="Cholesky" | custom-call | tf_op jit(solution)/shard_map/jit(cholesky)/cholesky | solution.py:41
  324.1 9.8 %custom-call.13 = f32[1,128,128]{1,2,0:T(8,128)S(1)} custom-call(f32[1,128,128]{2,1,0:T(8,128)S(1)} %get-tuple-element.58), custom_call_target="InvertDiagBlocksLowerTriangular" | custom-call | tf_op jit(solution)/shard_map/jit(cholesky)/cholesky | solution.py:41
  333.9 0.2 constant_dynamic-update-slice_fusion.3
  334.1 0.3 convolution_subtract_fusion.3
  334.4 11.7 %cholesky.147 = f32[128,128]{1,0:T(8,128)S(1)} custom-call(f32[128,128]{1,0:T(8,128)S(1)} %convolution_subtract_fusion.3), custom_call_target="Cholesky" | custom-call | tf_op jit(solution)/shard_map/jit(cholesky)/cholesky | solution.py:41
  346.1 0.7 compare_reduce_fusion.2
  346.8 0.6 compare_reduce_fusion.3
  348.9 4.1 while.4
  349.0 0.6 fusion.76
  349.6 1.4 bitcast_dynamic-update-slice_fusion.4
  351.0 0.6 fusion.76
  351.6 1.4 bitcast_dynamic-update-slice_fusion.4
  353.0 19.9 %custom-call.14 = f32[2,128,128]{1,2,0:T(8,128)S(1)} custom-call(f32[2,128,128]{2,1,0:T(8,128)S(1)} %get-tuple-element.21), custom_call_target="InvertDiagBlocksLowerTriangular" | custom-call | tf_op jit(solution)/shard_map/triangular_solve/custom-call.0 | solution.py:47
  372.9 0.3 fusion.8
  373.3 0.3 convolution_subtract_fusion.1
  373.5 0.3 fusion.17
  374.1 8.7 %copy.43 = f32[128,2,128,2]{3,2,1,0:T(8,128)} copy(f32[128,2,128,2]{2,0,3,1:T(8,128)S(1)} %pad_maximum_fusion.5) | data formatting | bytes 524288 | tf_op jit(solution)/shard_map/stack | solution.py:22
  382.8 12.7 %reshape.180 = f32[256,256]{1,0:T(8,128)S(1)} reshape(f32[128,2,128,2]{3,2,1,0:T(8,128)} %copy.43) | data formatting | bytes 524288 | tf_op jit(solution)/shard_map/reshape | solution.py:22
  395.7 11.7 %cholesky.164 = f32[128,128]{1,0:T(8,128)S(1)} custom-call(f32[128,128]{1,0:T(8,128)S(1)} %cholesky.197), custom_call_target="Cholesky" | custom-call | tf_op jit(solution)/shard_map/jit(cholesky)/cholesky | solution.py:41
  407.4 9.8 %custom-call.15 = f32[1,128,128]{1,2,0:T(8,128)S(1)} custom-call(f32[1,128,128]{2,1,0:T(8,128)S(1)} %get-tuple-element.64), custom_call_target="InvertDiagBlocksLowerTriangular" | custom-call | tf_op jit(solution)/shard_map/jit(cholesky)/cholesky | solution.py:41
  417.5 0.3 convolution_subtract_fusion.2
  417.7 11.7 %cholesky.181 = f32[128,128]{1,0:T(8,128)S(1)} custom-call(f32[128,128]{1,0:T(8,128)S(1)} %convolution_subtract_fusion.2), custom_call_target="Cholesky" | custom-call | tf_op jit(solution)/shard_map/jit(cholesky)/cholesky | solution.py:41
  429.5 0.7 compare_reduce_fusion
  430.2 0.6 compare_reduce_fusion.1
  432.2 4.1 while.5
  432.3 0.6 fusion.77
  432.9 1.4 bitcast_dynamic-update-slice_fusion.5
  434.3 0.6 fusion.77
  434.9 1.4 bitcast_dynamic-update-slice_fusion.5
  436.4 19.9 %custom-call.16 = f32[2,128,128]{1,2,0:T(8,128)S(1)} custom-call(f32[2,128,128]{2,1,0:T(8,128)S(1)} %get-tuple-element.22), custom_call_target="InvertDiagBlocksLowerTriangular" | custom-call | tf_op jit(solution)/shard_map/triangular_solve/custom-call.0 | solution.py:47
  456.3 0.3 fusion.6
  456.6 0.3 convolution_subtract_fusion
  456.9 0.3 fusion.11
  457.4 0.8 pad_maximum_fusion
  (56 shorter events, 3.2 us)
Async XLA Ops:
  6.5 1.7 copy-start
  9.5 15.3 %all-to-all-start = ((bf16[2,16,16,256]{3,2,0,1:T(8,128)(2,1)}), bf16[2,16,16,256]{3,2,0,1:T(8,128)(2,1)S(1)}, u32[]{:S(2)}, u32[]{:S(2)}) async-start(bf16[2,16,16,256]{3,2,0,1:T(8,128)(2,1)} %copy.34), calls=%async_computation | async-start | bytes 524288 | tf_op jit(solution)/shard_map/all_to_all | solution.py:67
  18.6 270.0 %all-reduce.3.cloned.1.call-start = ((), (), s32[]{:S(2)}) async-start(), calls=%async_computation.1 | async-start | bytes 524288 | tf_op jit(solution)/shard_map/psum | solution.py:75
Sparse Core Ops, SparseCore 0:
  26.9 261.7 all-reduce.2
where the time goes:
time: 466 us; the launch traced here: 465 us
  waiting for transfers between devices  267 us (57%)
  other arithmetic  115 us (25%)
  local copies, waits for them, and re-layouts  53.6 us (12%)
  between operations  16.5 us (4%)
  starting transfers between devices  9.15 us (2%)
    psum x1, waiting for transfers between devices, local(): summed = lax.psum(local_grams, 'space')  261 us
    another operation x14, other arithmetic, finish_modes(): lower_factor = jnp.linalg.cholesky(embedded)  69.3 us
    another operation x7, other arithmetic, finish_modes(): lax.linalg.triangular_solve(lower_factor, stacked_rows, left_side=True, l...  39.9 us
    reshape x4, local copies, waits for them, and re-layouts, embed_gram(): return jnp.stack([top_rows, low_rows], axis=1).reshape(2 * order, 2 * order)  25.6 us
    another operation x2, local copies, waits for them, and re-layouts, embed_gram(): return jnp.stack([top_rows, low_rows], axis=1).reshape(2 * order, 2 * order)  17.5 us
  transfers between devices with their start and end apart: 2, of which 2 were waited for; matrix products, arithmetic and copies ran while one was open for 0% of the time, Pallas kernels for 0%

commit v1 on v0

--- a/solution.py
+++ b/solution.py
@@ -3,6 +3,11 @@
 import jax.numpy as jnp
 from jax import lax
 from jax.sharding import PartitionSpec as P
+
+
+def _move_meshes(array_in, link_axis):
+    inter = lax.all_gather(array_in, axis_name=link_axis).sum(axis=0)
+    return inter
 
 
 def make_angle_table(frequencies, length):
@@ -72,7 +77,7 @@
         for slot_index in range(regrouped.shape[1])
     ]
     local_grams = jnp.stack([local_gram(real_rows, imag_rows) for real_rows, imag_rows in per_freq])
-    summed = lax.psum(local_grams, "space")
+    summed = _move_meshes(local_grams, link_axis="space")
     results = [
         finish_modes(
             summed[slot_index], per_freq[slot_index][0], per_freq[slot_index][1], total_cells

time: 466 us -> 401 us (0.86)
  the two profiles are of different devices: /device:TPU:8 before, /device:TPU:1 now
where the time goes in v1:
time: 401 us
  waiting for transfers between devices  192 us (48%)
  other arithmetic  120 us (30%)
  local copies, waits for them, and re-layouts  52.8 us (13%)
  between operations  16.5 us (4%)
  blocking collectives  15.8 us (4%)
    all_gather x1, waiting for transfers between devices, _move_meshes(): inter = lax.all_gather(array_in, axis_name=link_axis).sum(axis=0)  192 us
    another operation x14, other arithmetic, finish_modes(): lower_factor = jnp.linalg.cholesky(embedded)  69.3 us
    another operation x7, other arithmetic, finish_modes(): lax.linalg.triangular_solve(lower_factor, stacked_rows, left_side=True, l...  39.9 us
    reshape x4, local copies, waits for them, and re-layouts, embed_gram(): return jnp.stack([top_rows, low_rows], axis=1).reshape(2 * order, 2 * order)  25.8 us
    another operation x2, local copies, waits for them, and re-layouts, embed_gram(): return jnp.stack([top_rows, low_rows], axis=1).reshape(2 * order, 2 * order)  17.3 us
    all_to_all x1, blocking collectives, local(): lax.all_to_all(stacked, 'tm', split_axis=1, concat_axis=2, tiled=True)  15.8 us
    another operation x15, local copies, waits for them, and re-layouts, finish_modes(): lax.linalg.triangular_solve(lower_factor, stacked_rows, left_side=True, l...  8.21 us
  transfers between devices with their start and end apart: 1, of which 1 were waited for; matrix products, arithmetic and copies ran while one was open for 0% of the time, Pallas kernels for 0%

profile of v1, /device:TPU:1, one launch (start us, length us, event | category | flops | bytes accessed | tf_op | source)
XLA Modules:
  0.0 400.5 jit_solution(8221297225425109200)
XLA Ops:
  6.6 0.9 multiply_convert_fusion.1
  7.5 0.8 fusion.59
  8.3 0.3 fusion.52
  8.8 15.8 %all_to_all.18 = bf16[2,16,16,256]{3,2,0,1:T(8,128)(2,1)S(1)} all-to-all(bf16[2,16,16,256]{3,2,0,1:T(8,128)(2,1)S(1)} %copy.34), channel_id=1, replica_groups=mesh['tm'=8,'space'=64] {'tm'}, dimensions={1} | all-to-all | bytes 524288 | tf_op jit(solution)/shard_map/all_to_all | solution.py:72
  25.9 0.7 pad_maximum_fusion.2
  26.7 0.2 copy.41
  26.9 0.2 reshape.206
  27.1 0.2 copy.45
  27.3 0.2 reshape.207
  27.5 191.8 %all-gather.3.cloned.1.call-done = f32[128,2,128,128]{3,2,1,0:T(8,128)} async-done(((f32[2,2,128,128]{3,2,1,0:T(8,128)}), f32[128,2,128,128]{3,2,1,0:T(8,128)}) %all-gather.3.cloned.1.call-update) | async-done | bytes 16777232 | tf_op jit(solution)/shard_map/all_gather | solution.py:9
  219.3 6.6 %reduce_sum.9 = f32[2,2,128,128]{3,2,1,0:T(8,128)S(1)} reduce(f32[64,2,2,128,128]{4,3,2,1,0:T(8,128)} %bitcast.157, f32[]{:T(128)} %constant.90.clone.1), dimensions={0}, to_apply=%region_0.1 | reduce | flops 4128768 | bytes 17039364 | tf_op jit(solution)/shard_map/reduce_sum | solution.py:9
  226.0 8.7 %copy.39 = f32[128,2,128,2]{3,2,1,0:T(8,128)} copy(f32[128,2,128,2]{2,0,3,1:T(8,128)S(1)} %pad_maximum_fusion.3) | data formatting | bytes 524288 | tf_op jit(solution)/shard_map/stack | solution.py:27
  234.7 12.9 %reshape.178 = f32[256,256]{1,0:T(8,128)S(1)} reshape(f32[128,2,128,2]{3,2,1,0:T(8,128)} %copy.39) | data formatting | bytes 524288 | tf_op jit(solution)/shard_map/reshape | solution.py:27
  247.7 11.7 %cholesky.130 = f32[128,128]{1,0:T(8,128)S(1)} custom-call(f32[128,128]{1,0:T(8,128)S(1)} %cholesky.194), custom_call_target="Cholesky" | custom-call | tf_op jit(solution)/shard_map/jit(cholesky)/cholesky | solution.py:46
  259.5 9.8 %custom-call.13 = f32[1,128,128]{1,2,0:T(8,128)S(1)} custom-call(f32[1,128,128]{2,1,0:T(8,128)S(1)} %get-tuple-element.58), custom_call_target="InvertDiagBlocksLowerTriangular" | custom-call | tf_op jit(solution)/shard_map/jit(cholesky)/cholesky | solution.py:46
  269.3 0.2 constant_dynamic-update-slice_fusion.3
  269.5 0.3 convolution_subtract_fusion.3
  269.8 11.7 %cholesky.147 = f32[128,128]{1,0:T(8,128)S(1)} custom-call(f32[128,128]{1,0:T(8,128)S(1)} %convolution_subtract_fusion.3), custom_call_target="Cholesky" | custom-call | tf_op jit(solution)/shard_map/jit(cholesky)/cholesky | solution.py:46
  281.6 0.7 compare_reduce_fusion.2
  282.3 0.6 compare_reduce_fusion.3
  284.4 4.1 %while.4 = (s32[]{:T(128)}, f32[256,256]{1,0:T(8,128)S(1)}, s32[2,2]{1,0:T(2,128)S(1)}, f32[2,128,128]{2,1,0:T(8,128)S(1)}, s32[]{:T(128)}) while((s32[]{:T(128)}, f32[256,256]{1,0:T(8,128)S(1)}, s32[2,2]{1,0:T(2,128)S(1)}, f32[2,128,128]{2,1,0:T(8,128)S(1)}, s32[]{:T(128)}) %tuple.59), condition=%wide.while_cond, body=%wide.while_body.sunk | while | flops 2 | bytes 131181 | solution.py:52
  284.4 0.6 fusion.76
  285.0 1.4 bitcast_dynamic-update-slice_fusion.4
  286.5 0.6 fusion.76
  287.1 1.4 bitcast_dynamic-update-slice_fusion.4
  288.5 19.9 %custom-call.14 = f32[2,128,128]{1,2,0:T(8,128)S(1)} custom-call(f32[2,128,128]{2,1,0:T(8,128)S(1)} %get-tuple-element.21), custom_call_target="InvertDiagBlocksLowerTriangular" | custom-call | tf_op jit(solution)/shard_map/triangular_solve/custom-call.0 | solution.py:52
  308.4 0.3 fusion.8
  308.7 0.3 convolution_subtract_fusion.1
  309.0 0.3 fusion.17
  309.6 8.7 %copy.43 = f32[128,2,128,2]{3,2,1,0:T(8,128)} copy(f32[128,2,128,2]{2,0,3,1:T(8,128)S(1)} %pad_maximum_fusion.5) | data formatting | bytes 524288 | tf_op jit(solution)/shard_map/stack | solution.py:27
  318.2 12.7 %reshape.180 = f32[256,256]{1,0:T(8,128)S(1)} reshape(f32[128,2,128,2]{3,2,1,0:T(8,128)} %copy.43) | data formatting | bytes 524288 | tf_op jit(solution)/shard_map/reshape | solution.py:27
  331.1 11.7 %cholesky.164 = f32[128,128]{1,0:T(8,128)S(1)} custom-call(f32[128,128]{1,0:T(8,128)S(1)} %cholesky.197), custom_call_target="Cholesky" | custom-call | tf_op jit(solution)/shard_map/jit(cholesky)/cholesky | solution.py:46
  342.9 9.8 %custom-call.15 = f32[1,128,128]{1,2,0:T(8,128)S(1)} custom-call(f32[1,128,128]{2,1,0:T(8,128)S(1)} %get-tuple-element.64), custom_call_target="InvertDiagBlocksLowerTriangular" | custom-call | tf_op jit(solution)/shard_map/jit(cholesky)/cholesky | solution.py:46
  352.7 0.2 constant_dynamic-update-slice_fusion.1
  352.9 0.3 convolution_subtract_fusion.2
  353.2 11.7 %cholesky.181 = f32[128,128]{1,0:T(8,128)S(1)} custom-call(f32[128,128]{1,0:T(8,128)S(1)} %convolution_subtract_fusion.2), custom_call_target="Cholesky" | custom-call | tf_op jit(solution)/shard_map/jit(cholesky)/cholesky | solution.py:46
  364.9 0.7 compare_reduce_fusion
  365.7 0.6 compare_reduce_fusion.1
  367.7 4.1 %while.5 = (s32[]{:T(128)}, f32[256,256]{1,0:T(8,128)S(1)}, s32[2,2]{1,0:T(2,128)S(1)}, f32[2,128,128]{2,1,0:T(8,128)S(1)}, s32[]{:T(128)}) while((s32[]{:T(128)}, f32[256,256]{1,0:T(8,128)S(1)}, s32[2,2]{1,0:T(2,128)S(1)}, f32[2,128,128]{2,1,0:T(8,128)S(1)}, s32[]{:T(128)}) %tuple.64), condition=%wide.while_cond.clone, body=%wide.while_body.clone.sunk | while | flops 2 | bytes 131181 | solution.py:52
  367.7 0.6 fusion.77
  368.3 1.4 bitcast_dynamic-update-slice_fusion.5
  369.8 0.6 fusion.77
  370.4 1.4 bitcast_dynamic-update-slice_fusion.5
  371.8 19.9 %custom-call.16 = f32[2,128,128]{1,2,0:T(8,128)S(1)} custom-call(f32[2,128,128]{2,1,0:T(8,128)S(1)} %get-tuple-element.22), custom_call_target="InvertDiagBlocksLowerTriangular" | custom-call | tf_op jit(solution)/shard_map/triangular_solve/custom-call.0 | solution.py:52
  391.8 0.3 fusion.6
  392.1 0.3 convolution_subtract_fusion
  392.3 0.3 fusion.11
  392.9 0.8 pad_maximum_fusion
  (56 shorter events, 2.8 us)
Async XLA Ops:
  6.5 1.7 copy-start
  6.5 212.7 %all-gather.3.cloned.1.call-start = ((), (), s32[]{:S(2)}) async-start(), calls=%async_computation.1 | async-start | bytes 17039360 | tf_op jit(solution)/shard_map/all_gather | solution.py:9
Sparse Core Ops, SparseCore 0:
  26.7 192.4 all-gather.2
